TPU v7x, 512 devices: a whole 4x8x8 slice. The times are simulated.
512 devices in a mesh: scen: 8 (over y), blk: 64 (over z, x, core).
Axes of the slice: x: 4, y: 8, z: 8, core: 2. Of those that a mesh axis runs over, the one named last changes fastest.
Arguments:
- returns: bfloat16 [512, 32768], P(('scen', 'blk')), may hold values from -6 to 6
- vol_hist: float32 [512, 32768], P(('scen', 'blk')), may hold values from 0.5 to 5.5, as said below
- vol_now: float32 [32768], replicated, may hold values from 0.5 to 2
- sensitivity: bfloat16 [16384, 128, 128], P('blk'), may hold values from -0.109375 to 0.109375
- block_pairs: int32 [16384, 3], P('blk'), may hold values from 0 to 255, as said below
- book_order: int32 [128], replicated, may hold values from 0 to 127, each once
Outputs:
- profit_loss: float32 [512, 16384], P('scen', 'blk')
- book_rms: float32 [16384], P('blk')
Inputs may be any that keep to these rules, and one draw needn't show every extreme that they name: `block_pairs`: each index k of blk holds 256 slots; their factor blocks lie in k * 4 to k * 4 + 3; on each index the live slots come first; some index has all 256 slots live. `vol_hist`: positive volatilities.
All inputs are finite; a program needn't handle non-finite values.
Results may differ from a plain program's by a relative error of at most 0.0029.
Values may be sent and summed in bfloat16 or wider, within the bound.
A program may use at most 64 MiB of HBM per device.

v0:
```python
import jax
import jax.numpy as jnp
from jax import lax
from jax.sharding import PartitionSpec as P


def shards(returns, vol_hist, vol_now, sensitivity, block_pairs, book_order):
    rescaled = (returns.astype(jnp.float32) * vol_now[None, :] / vol_hist).astype(jnp.bfloat16)
    groups = lax.axis_size("blk")
    column = lax.axis_index("blk")
    block_size = sensitivity.shape[1]
    own_width = rescaled.shape[1] // groups
    gathered = lax.all_gather(rescaled, "blk", axis=0, tiled=True)
    own_shocks = lax.dynamic_slice_in_dim(gathered, column * own_width, own_width, 1)
    scen_rows = own_shocks.shape[0]
    local_blocks = own_shocks.reshape(scen_rows, own_width // block_size, block_size)
    factor_local = block_pairs[:, 0] - column * (own_width // block_size)
    picked = jnp.take(local_blocks, factor_local, axis=1)
    products = jnp.einsum("skc,kcd->ksd", picked, sensitivity, preferred_element_type=jnp.float32)
    book_blocks = book_order.shape[0]
    matches = book_order[None, :] == block_pairs[:, 1][:, None]
    position = jnp.sum(
        jnp.where(matches, jnp.arange(book_blocks, dtype=jnp.int32)[None, :], 0), axis=1
    )
    live_weight = block_pairs[:, 2].astype(jnp.float32)
    selector = jnp.where(
        jnp.arange(book_blocks, dtype=jnp.int32)[:, None] == position[None, :],
        live_weight[None, :],
        0.0,
    )
    partial_sum = jnp.einsum("bk,ksd->bsd", selector, products, precision=lax.Precision.HIGHEST)
    owned_books = lax.psum_scatter(partial_sum, "blk", scatter_dimension=0, tiled=True)
    profit_loss = owned_books.transpose(1, 0, 2).reshape(scen_rows, -1)
    squares = lax.psum(jnp.sum(profit_loss * profit_loss, axis=0), "scen")
    total_rows = scen_rows * lax.axis_size("scen")
    book_rms = jnp.sqrt(squares / total_rows + 1e-06)
    return (profit_loss, book_rms)


def solution(mesh):
    return jax.shard_map(
        shards,
        mesh=mesh,
        in_specs=(
            P(("scen", "blk"), None),
            P(("scen", "blk"), None),
            P(),
            P("blk", None, None),
            P("blk", None),
            P(),
        ),
        out_specs=(P("scen", "blk"), P("blk")),
        check_vma=False,
    )
```

profile of v0, /device:TPU:2, one launch (start us, length us, event | category | flops | bytes accessed | tf_op | source)
XLA Modules:
  0.0 306.9 jit_solution(5500297832278596794)
XLA Ops:
  7.2 0.0 all-gather.3.cloned.1.call-start
  7.2 1.9 convert_bitcast_fusion
  9.1 0.0 all-gather.3.cloned.1.call-update
  9.1 0.0 reduce-scatter.2.cloned.1.call-start
  9.2 0.7 and_reduce_fusion
  9.9 0.8 fusion.15
  10.7 0.8 select_reduce_fusion
  11.5 93.0 %all-gather.3.cloned.1.call-done = bf16[64,1,32768]{2,1,0:T(2,128)(2,1)} async-done(((bf16[1,1,32768]{2,1,0:T(2,128)(2,1)}), bf16[64,1,32768]{2,1,0:T(2,128)(2,1)}) %all-gather.3.cloned.1.call-update) | async-done | bytes 4194320 | tf_op jit(solution)/shard_map/all_gather | solution.py:13
  104.5 1.3 dynamic-slice_reduce_fusion
  105.8 3.0 gather_fusion
  108.8 7.0 %fusion.2 = f32[256,64,128]{2,1,0:T(8,128)S(1)} fusion(bf16[256,128,128]{2,1,0:T(8,128)(2,1)} %param.9, bf16[256,64,128]{2,1,0:T(8,128)(2,1)} %gather_fusion, pred[256]{0:T(512)(128)(4,1)S(1)} %get-tuple-element.2), kind=kOutput, calls=%fused_computation.3 | convolution fusion | flops 538968064 | bytes 20971776 | tf_op jit(solution)/shard_map/skc,kcd->ksd/dot_general | solution.py:19
  115.9 10.2 %fusion = f32[128,64,128]{2,0,1:T(8,128)S(1)} fusion(f32[256,64,128]{2,1,0:T(8,128)S(1)} %fusion.2, f32[256]{0:T(256)S(1)} %bitcast.32, s32[256]{0:T(256)S(1)} %select_reduce_fusion), kind=kOutput, calls=%fused_computation.1 | convolution fusion | flops 3221291008 | bytes 12584960 | tf_op jit(solution)/shard_map/bk,ksd->bsd/dot_general | solution.py:31
  126.1 4.4 %copy.18 = f32[128,64,128]{2,1,0:T(8,128)} copy(f32[128,64,128]{2,0,1:T(8,128)S(1)} %fusion) | data formatting | bytes 8388608 | tf_op jit(solution)/shard_map/bk,ksd->bsd/dot_general | solution.py:31
  130.4 0.0 reduce-scatter.2.cloned.1.call-update
  130.5 149.7 %reduce-scatter.2.cloned.1.call-done = f32[2,64,128]{2,1,0:T(8,128)} async-done(((f32[128,64,128]{2,1,0:T(8,128)}), f32[2,64,128]{2,1,0:T(8,128)}) %reduce-scatter.2.cloned.1.call-update) | async-done | bytes 65552 | tf_op jit(solution)/shard_map/reduce_scatter | solution.py:32
  280.2 0.9 fusion.9
  281.1 17.0 %psum.7 = f32[256]{0:T(256)S(1)} all-reduce(f32[256]{0:T(256)S(1)} %bitcast.29), channel_id=1, replica_groups=mesh['scen'=8,'blk'=64] {'scen'}, use_global_device_ids=true, to_apply=%region_3.4 | all-reduce | flops 256 | bytes 2048 | tf_op jit(solution)/shard_map/psum | solution.py:34
  298.0 0.6 add_sqrt_fusion
  298.6 1.5 copy_bitcast_fusion
  (2 shorter events, 0.0 us)
Async XLA Ops:
  7.2 97.4 %all-gather.3.cloned.1.call-start = ((), (), s32[]{:S(2)}) async-start(), calls=%async_computation.2 | async-start | bytes 8519680 | tf_op jit(solution)/shard_map/all_gather | solution.py:13
  9.1 271.0 %reduce-scatter.2.cloned.1.call-start = ((), (), s32[]{:S(2)}) async-start(), calls=%async_computation.1 | async-start | bytes 4259840 | tf_op jit(solution)/shard_map/reduce_scatter | solution.py:32
Sparse Core Ops, SparseCore 0:
  11.3 93.1 all-gather.2
  130.6 149.5 reduce-scatter.1
where the time goes:
time: 307 us
  waiting for transfers between devices  243 us (79%)
  matrix products  17.2 us (6%)
  blocking collectives  17 us (6%)
  between operations  14.1 us (5%)
  local copies, waits for them, and re-layouts  10.1 us (3%)
  other arithmetic  5.67 us (2%)
    reduce_scatter x1, waiting for transfers between devices, shards(): lax.psum_scatter(partial_sum, 'blk', scatter_dimension=0, tiled=True)  150 us
    all_gather x1, waiting for transfers between devices, shards(): gathered = lax.all_gather(rescaled, 'blk', axis=0, tiled=True)  93 us
    psum x1, blocking collectives, shards(): squares = lax.psum(jnp.sum(profit_loss * profit_loss, axis=0), 'scen')  17 us
    dot_general x1, matrix products, shards(): jnp.einsum('bk,ksd->bsd', selector, products, precision=lax.Precision.HIG...  10.2 us
    dot_general x1, matrix products, shards(): jnp.einsum('skc,kcd->ksd', picked, sensitivity, preferred_element_type=jn...  7.02 us
  transfers between devices with their start and end apart: 2, of which 2 were waited for; matrix products, arithmetic and copies ran while one was open for 1% of the time, Pallas kernels for 0%

commit v1 on v0

v1 whole, which is shorter than its diff:
```python
import functools

import jax
import jax.numpy as jnp
from jax import lax
from jax.experimental import pallas as pl
from jax.experimental.pallas import tpu as pltpu
from jax.sharding import PartitionSpec as P

MESH = pl.DeviceIdType.MESH
F32 = jnp.float32
BF16 = jnp.bfloat16
NX = 4
NC = 2
LANES = 128


def remote(src, dst, send, recv, **where):
    return pltpu.make_async_remote_copy(
        src_ref=src, dst_ref=dst, send_sem=send, recv_sem=recv, device_id=where, device_id_type=MESH
    )


def iota(shape, axis):
    return lax.broadcasted_iota(jnp.int32, shape, axis).astype(F32)


def to_column(row):
    n = row.shape[1]
    eye = lax.broadcasted_iota(jnp.int32, (n, n), 0) == lax.broadcasted_iota(jnp.int32, (n, n), 1)
    return jnp.sum(jnp.where(eye, jnp.broadcast_to(row, (n, n)), 0.0), axis=1, keepdims=True)


def sort_slots(pairs, order, first_factor):
    slots, blocks = pairs.shape[1], order.shape[1]
    pairs = pairs.astype(F32)
    factor = pairs[0:1] - first_factor.astype(F32)
    matches = to_column(order.astype(F32)) == pairs[1:2]
    position = jnp.sum(jnp.where(matches, iota((blocks, slots), 0), 0.0), axis=0, keepdims=True)
    position = jnp.where(pairs[2:3] > 0.5, position, float(blocks))
    value = (position * slots + iota((1, slots), 1)) * 4.0 + factor
    value_col = to_column(value)
    position_col = to_column(position)
    rank_col = jnp.sum(jnp.where(value < value_col, 1.0, 0.0), axis=1, keepdims=True)
    ordered = jnp.sum(jnp.where(rank_col == iota((slots, slots), 1), value_col, 0.0), axis=0, keepdims=True)
    columns = iota((slots, blocks), 1)
    upto = jnp.sum(jnp.where(position_col <= columns, 1.0, 0.0), axis=0, keepdims=True)
    here = jnp.sum(jnp.where(position_col == columns, 1.0, 0.0), axis=0, keepdims=True)
    last = jnp.maximum(upto - 1.0, 0.0) * 2.0 + jnp.minimum(here, 1.0)
    return ordered.astype(jnp.int32), last.astype(jnp.int32)


def kernel(
    ny, nz, dz_order,
    row_ref, pairs_ref, order_ref, sens_ref,
    out_ref, rms_ref,
    sens_v, land1, turned, shocks_f, shocks_b, running, give, got0, part_x, got1, part_z, got2, mine,
    squares, got3, ordered_v, last_v, ordered_s, last_s,
    sens_sem, meta_sem, send1, recv1, send2, recv2, send_c, recv_c, send_x, recv_x, send_z, recv_z, send_y, recv_y,
):
    nq = NX * NC
    slots = sens_v.shape[0]
    rows = nz * nq
    me_y = lax.axis_index("scen")
    me = lax.axis_index("blk")
    z, q = me // nq, me % nq
    x, c = q // NC, q % NC
    fb = shocks_f.shape[1]

    pieces = sens_sem.shape[0]
    each = slots // pieces
    loads = [
        pltpu.make_async_copy(sens_ref.at[pl.ds(i * each, each)], sens_v.at[pl.ds(i * each, each)], sens_sem.at[i])
        for i in range(pieces)
    ]
    for load in loads:
        load.start()

    barrier = pltpu.get_barrier_semaphore()
    for d in range(1, nz):
        pl.semaphore_signal(barrier, 1, device_id={"blk": lax.rem(z + d, nz) * nq + q}, device_id_type=MESH)
    for d in range(1, nq):
        pl.semaphore_signal(barrier, 1, device_id={"blk": z * nq + lax.rem(q + d, nq)}, device_id_type=MESH)
    for d in range(1, ny):
        pl.semaphore_signal(barrier, 1, device_id={"scen": lax.rem(me_y + d, ny)}, device_id_type=MESH)
    pl.semaphore_wait(barrier, nz - 1 + nq - 1 + ny - 1)

    slab = nq * fb
    stage1 = []
    for d in range(1, nz):
        to = lax.rem(z + d, nz)
        stage1.append(
            remote(row_ref.at[to], land1.at[z], send1.at[d - 1], recv1.at[d - 1], blk=to * nq + q)
        )
    for copy in stage1:
        copy.start()
    land1[pl.ds(z, 1)] = row_ref[pl.ds(z, 1)]

    ordered, last = sort_slots(pairs_ref[...], order_ref[...], me * fb)
    ordered_v[...] = ordered
    last_v[...] = last
    metas = [
        pltpu.make_async_copy(ordered_v, ordered_s, meta_sem.at[0]),
        pltpu.make_async_copy(last_v, last_s, meta_sem.at[1]),
    ]
    for copy in metas:
        copy.start()

    for copy in stage1:
        copy.wait_recv()
    turned[...] = jnp.swapaxes(land1[...].astype(F32), 0, 1).reshape(nq, fb, nz, LANES)
    stage2 = []
    for d in range(1, nq):
        to = lax.rem(q + d, nq)
        stage2.append(
            remote(turned.at[to], shocks_f.at[q], send2.at[d - 1], recv2.at[d - 1], blk=z * nq + to)
        )
    for copy in stage2:
        copy.start()
    shocks_f[pl.ds(q, 1)] = turned[pl.ds(q, 1)]
    for copy in metas:
        copy.wait()
    for load in loads:
        load.wait()
    for copy in stage2:
        copy.wait_recv()
    for f in range(fb):
        shocks_b[f] = shocks_f[:, f].reshape(rows, LANES).astype(BF16)

    unroll = 8
    slot_bits = slots.bit_length() - 1

    def slot_group(g, carry):
        total, before = carry
        for u in range(unroll):
            j = g * unroll + u
            value = ordered_s[0, j]
            factor = value & 3
            k = (value >> 2) & (slots - 1)
            position = value >> (2 + slot_bits)
            product = jnp.dot(shocks_b[factor], sens_v[k], preferred_element_type=F32)
            same = (position == before).astype(F32)
            total = total * same + product
            running[j] = total
            before = position
        return total, before

    lax.fori_loop(0, slots // unroll, slot_group, (jnp.zeros((rows, LANES), F32), jnp.int32(-1)))

    def partial_of(p):
        value = last_s[0, p]
        return running[(value >> 1) & (slots - 1)] * (value & 1).astype(F32)

    chunks = len(dz_order)
    core_copies, x_copies, z_copies = [], [], []
    for i, dz in enumerate(dz_order):
        to_z = lax.rem(z + dz, nz)
        for to_x in range(NX):
            for h in range(2):
                give[i, to_x, h] = partial_of(((to_z * NX + to_x) * NC + (1 - c)) * 2 + h)
        copy = remote(give.at[i], got0.at[i], send_c.at[i], recv_c.at[i], blk=z * nq + x * NC + (1 - c))
        copy.start()
        core_copies.append(copy)

    for i in range(chunks + 1):
        if i < chunks:
            dz = dz_order[i]
            to_z = lax.rem(z + dz, nz)
            core_copies[i].wait_recv()
            group = []
            for d in range(NX):
                to_x = lax.rem(x + d, NX)
                for h in range(2):
                    total = got0[i, to_x, h] + partial_of(((to_z * NX + to_x) * NC + c) * 2 + h)
                    if d == 0:
                        mine[i % 2, h] = total
                    else:
                        part_x[i, d - 1, h] = total.astype(BF16)
                if d > 0:
                    copy = remote(
                        part_x.at[i, d - 1], got1.at[i, d - 1], send_x.at[i, d - 1], recv_x.at[i, d - 1],
                        blk=(z * NX + to_x) * NC + c,
                    )
                    copy.start()
                    group.append(copy)
            x_copies.append(group)
        if i > 0:
            e = i - 1
            dz = dz_order[e]
            for copy in x_copies[e]:
                copy.wait_recv()
            for h in range(2):
                total = mine[e % 2, h]
                for d in range(NX - 1):
                    total = total + got1[e, d, h].astype(F32)
                if dz == 0:
                    mine[e % 2, h] = total
                else:
                    part_z[e, h] = total.astype(BF16)
            if dz != 0:
                copy = remote(
                    part_z.at[e], got2.at[e], send_z.at[e], recv_z.at[e],
                    blk=lax.rem(z + dz, nz) * nq + q,
                )
                copy.start()
                z_copies.append(copy)
    for copy in z_copies:
        copy.wait_recv()
    for h in range(2):
        total = mine[(chunks - 1) % 2, h]
        for e in range(chunks - 1):
            total = total + got2[e, h].astype(F32)
        squares[0, h:h + 1] = jnp.sum(total * total, axis=0, keepdims=True)
        total = jnp.swapaxes(total.reshape(nq, nz, LANES), 0, 1)
        out_ref[:, h * LANES:(h + 1) * LANES] = total.reshape(rows, LANES)
    y_copies = []
    for d in range(1, ny):
        copy = remote(
            squares.at[0], got3.at[d - 1], send_y.at[d - 1], recv_y.at[d - 1], scen=lax.rem(me_y + d, ny)
        )
        copy.start()
        y_copies.append(copy)
    for copy in y_copies:
        copy.wait_recv()
    total = squares[0]
    for d in range(ny - 1):
        total = total + got3[d]
    rms_ref[...] = jnp.sqrt(total / (rows * ny) + 1e-06)
    for copy in stage1 + stage2 + core_copies + z_copies + y_copies:
        copy.wait_send()
    for group in x_copies:
        for copy in group:
            copy.wait_send()


def shards(ny, nz, returns, vol_hist, vol_now, sensitivity, block_pairs, book_order):
    rescaled = (returns.astype(F32) * vol_now[None, :] / vol_hist).astype(BF16)
    nq = NX * NC
    slots = sensitivity.shape[0]
    blocks = book_order.shape[0]
    fb = rescaled.shape[1] // (nz * nq * LANES)
    rows = nz * nq
    row = rescaled.reshape(nz, nq * fb, LANES)
    near = sorted(range(nz), key=lambda d: (-min(d, nz - d), d))
    dma = pltpu.SemaphoreType.DMA
    vm = pltpu.VMEM
    block = (rows, LANES)
    out, rms = pl.pallas_call(
        functools.partial(kernel, ny, nz, near),
        out_shape=(
            jax.ShapeDtypeStruct((rows, 2 * LANES), F32),
            jax.ShapeDtypeStruct((2, LANES), F32),
        ),
        in_specs=[
            pl.BlockSpec(memory_space=pltpu.VMEM),
            pl.BlockSpec(memory_space=pltpu.VMEM),
            pl.BlockSpec(memory_space=pltpu.VMEM),
            pl.BlockSpec(memory_space=pl.ANY),
        ],
        out_specs=(pl.BlockSpec(memory_space=pltpu.VMEM), pl.BlockSpec(memory_space=pltpu.VMEM)),
        scratch_shapes=[
            vm((slots, LANES, LANES), BF16),
            vm((nz, nq * fb, LANES), BF16),
            vm((nq, fb, nz, LANES), F32),
            vm((nq, fb, nz, LANES), F32),
            vm((fb,) + block, BF16),
            vm((slots,) + block, F32),
            vm((nz, NX, 2) + block, F32),
            vm((nz, NX, 2) + block, F32),
            vm((nz, NX - 1, 2) + block, BF16),
            vm((nz, NX - 1, 2) + block, BF16),
            vm((nz - 1, 2) + block, BF16),
            vm((nz - 1, 2) + block, BF16),
            vm((2, 2) + block, F32),
            vm((1, 2, LANES), F32),
            vm((ny - 1, 2, LANES), F32),
            vm((1, slots), jnp.int32),
            vm((1, blocks), jnp.int32),
            pltpu.SMEM((1, slots), jnp.int32),
            pltpu.SMEM((1, blocks), jnp.int32),
            dma((8,)),
            dma((2,)),
            dma((nz - 1,)),
            dma((nz - 1,)),
            dma((nq - 1,)),
            dma((nq - 1,)),
            dma((nz,)),
            dma((nz,)),
            dma((nz, NX - 1)),
            dma((nz, NX - 1)),
            dma((nz - 1,)),
            dma((nz - 1,)),
            dma((ny - 1,)),
            dma((ny - 1,)),
        ],
        compiler_params=pltpu.CompilerParams(
            collective_id=0, has_side_effects=True, vmem_limit_bytes=48 << 20
        ),
        name="profit_loss",
    )(row, block_pairs.T, book_order.reshape(1, blocks), sensitivity)
    return out, rms.reshape(2 * LANES)


def solution(mesh):
    ny, nb = mesh.shape["scen"], mesh.shape["blk"]
    return jax.shard_map(
        functools.partial(shards, ny, nb // (NX * NC)),
        mesh=mesh,
        in_specs=(
            P(("scen", "blk"), None),
            P(("scen", "blk"), None),
            P(),
            P("blk", None, None),
            P("blk", None),
            P(),
        ),
        out_specs=(P("scen", "blk"), P("blk")),
        check_vma=False,
    )
```

time: 307 us -> 61.5 us (0.20)
  the two profiles are of different devices: /device:TPU:2 before, /device:TPU:8 now
where the time goes in v1:
time: 61.5 us; the launch traced here: 61.3 us
  Pallas kernels  56.6 us (92%)
  local copies, waits for them, and re-layouts  2.53 us (4%)
  other arithmetic  1.49 us (2%)
  between operations  0.65 us (1%)
    pallas_call x1, Pallas kernels, shards(): pl.pallas_call(functools.partial(kernel, ny, nz, near), out_shape=(jax.Sh...  56.6 us
    unnamed x6, local copies, waits for them, and re-layouts  2.53 us
    convert_element_type x1, other arithmetic, shards(): rescaled = (returns.astype(F32) * vol_now[None, :] / vol_hist).astype(BF16)  1.49 us

profile of v1, /device:TPU:8, one launch (start us, length us, event | category | flops | bytes accessed | tf_op | source)
XLA Modules:
  0.0 61.3 jit_solution(14261213562621310703)
XLA Ops:
  0.6 1.5 %convert_reduce_fusion = bf16[32768]{0:T(1024)(128)(2,1)S(1)} fusion(f32[1,32768]{1,0:T(1,128)} %param.7, f32[1,32768]{1,0:T(1,128)} %bitcast.9, bf16[1,32768]{1,0:T(2,128)(2,1)} %param.6), kind=kLoop, calls=%fused_computation | loop fusion | flops 131072 | bytes 393216 | tf_op jit(solution)/shard_map/convert_element_type | solution.py:237
  2.1 0.0 copy-start
  2.1 0.7 %copy-done = s32[256,3]{0,1:T(4,128)S(1)} copy-done((s32[256,3]{0,1:T(4,128)S(1)}, s32[256,3]{0,1:T(4,128)}, u32[]{:S(2)}) %copy-start) | copy-done | bytes 3096
  2.8 0.0 copy-start.1
  2.8 0.7 %copy-done.1 = s32[128]{0:T(128)S(1)} copy-done((s32[128]{0:T(128)S(1)}, s32[128]{0:T(128)}, u32[]{:S(2)}) %copy-start.1) | copy-done | bytes 536
  3.5 56.6 %profit_loss.1 = (f32[64,256]{1,0:T(8,128)S(1)}, f32[2,128]{1,0:T(2,128)S(1)}) custom-call(bf16[8,32,128]{2,1,0:T(8,128)(2,1)S(1)} %bitcast.5, s32[3,256]{1,0:T(4,128)S(1)} %bitcast.6, s32[1,128]{1,0:T(1,128)S(1)} %bitcast.8, bf16[256,128,128]{2,1,0:T(8,128)(2,1)} %sens_ref.1), custom_call_target="tpu_custom_call" | custom-call | tf_op jit(solution)/shard_map/profit_loss/pallas_call | solution.py:248
  60.1 0.6 %copy.10 = f32[64,256]{1,0:T(8,128)} copy(f32[64,256]{1,0:T(8,128)S(1)} %get-tuple-element.8) | data formatting | bytes 131072
  60.7 0.6 copy.11
Async XLA Ops:
  2.1 0.7 %copy-start = (s32[256,3]{0,1:T(4,128)S(1)}, s32[256,3]{0,1:T(4,128)}, u32[]{:S(2)}) copy-start(s32[256,3]{0,1:T(4,128)} %param.10) | copy-start | bytes 9220
  2.8 0.7 %copy-start.1 = (s32[128]{0:T(128)S(1)}, s32[128]{0:T(128)}, u32[]{:S(2)}) copy-start(s32[128]{0:T(128)} %param.11) | copy-start | bytes 1540

commit v2 on v1

v2 whole, which is shorter than its diff:
```python
import functools

import jax
import jax.numpy as jnp
from jax import lax
from jax.experimental import pallas as pl
from jax.experimental.pallas import tpu as pltpu
from jax.sharding import PartitionSpec as P

MESH = pl.DeviceIdType.MESH
F32 = jnp.float32
BF16 = jnp.bfloat16
NX = 4
NC = 2
LANES = 128


def remote(src, dst, send, recv, **where):
    return pltpu.make_async_remote_copy(
        src_ref=src, dst_ref=dst, send_sem=send, recv_sem=recv, device_id=where, device_id_type=MESH
    )


def far_first(n):
    return sorted(range(1, n), key=lambda d: (-min(d, n - d), d))


def iota(shape, axis):
    return lax.broadcasted_iota(jnp.int32, shape, axis).astype(F32)


def to_column(row):
    n = row.shape[1]
    eye = lax.broadcasted_iota(jnp.int32, (n, n), 0) == lax.broadcasted_iota(jnp.int32, (n, n), 1)
    return jnp.sum(jnp.where(eye, jnp.broadcast_to(row, (n, n)), 0.0), axis=1, keepdims=True)


def sort_slots(pairs, order, first_factor):
    slots, blocks = pairs.shape[1], order.shape[1]
    pairs = pairs.astype(F32)
    factor = pairs[0:1] - first_factor.astype(F32)
    matches = to_column(order.astype(F32)) == pairs[1:2]
    position = jnp.sum(jnp.where(matches, iota((blocks, slots), 0), 0.0), axis=0, keepdims=True)
    position = jnp.where(pairs[2:3] > 0.5, position, float(blocks))
    value = (position * slots + iota((1, slots), 1)) * 4.0 + factor
    value_col = to_column(value)
    position_col = to_column(position)
    rank_col = jnp.sum(jnp.where(value < value_col, 1.0, 0.0), axis=1, keepdims=True)
    ordered = jnp.sum(jnp.where(rank_col == iota((slots, slots), 1), value_col, 0.0), axis=0, keepdims=True)
    columns = iota((slots, blocks), 1)
    upto = jnp.sum(jnp.where(position_col <= columns, 1.0, 0.0), axis=0, keepdims=True)
    here = jnp.sum(jnp.where(position_col == columns, 1.0, 0.0), axis=0, keepdims=True)
    last = jnp.maximum(upto - 1.0, 0.0) * 2.0 + jnp.minimum(here, 1.0)
    return ordered.astype(jnp.int32), last.astype(jnp.int32)


def kernel(
    ny, nz, dz_order,
    returns_ref, hist_ref, now_ref, pairs_ref, order_ref, sens_ref,
    out_ref, rms_ref,
    returns_v, hist_v, now_v, pairs_v, order_v, wide, row_ref,
    sens_v, land1, gathered, shocks_b, running, give, got0, part_r, got_r, held, part_x, got1, part_z, got2, mine,
    squares, got3, ordered_v, last_v, ordered_s, last_s,
    in_sem, sens_sem, meta_sem, send1, recv1, send2, recv2, send_c, recv_c, send_r, recv_r, send_x, recv_x, send_z, recv_z, send_y, recv_y,
):
    nq = NX * NC
    slots = sens_v.shape[0]
    rows = nz * nq
    me_y = lax.axis_index("scen")
    me = lax.axis_index("blk")
    z, q = me // nq, me % nq
    x, c = q // NC, q % NC
    fb = shocks_b.shape[0]

    barrier = pltpu.get_barrier_semaphore()
    for d in far_first(nz):
        pl.semaphore_signal(barrier, 1, device_id={"blk": lax.rem(z + d, nz) * nq + q}, device_id_type=MESH)
    for d in far_first(ny):
        pl.semaphore_signal(barrier, 1, device_id={"scen": lax.rem(me_y + d, ny)}, device_id_type=MESH)
    for d in range(1, nq):
        pl.semaphore_signal(barrier, 1, device_id={"blk": z * nq + lax.rem(q + d, nq)}, device_id_type=MESH)

    inputs = [
        pltpu.make_async_copy(src, dst, in_sem.at[i])
        for i, (src, dst) in enumerate((
            (returns_ref, returns_v), (hist_ref, hist_v), (now_ref, now_v), (pairs_ref, pairs_v), (order_ref, order_v)
        ))
    ]
    for copy in inputs:
        copy.start()
    pieces = sens_sem.shape[0]
    each = slots // pieces
    loads = [
        pltpu.make_async_copy(sens_ref.at[pl.ds(i * each, each)], sens_v.at[pl.ds(i * each, each)], sens_sem.at[i])
        for i in range(pieces)
    ]
    for copy in inputs:
        copy.wait()
    for load in loads:
        load.start()

    for i in range(rows * fb):
        wide[i // fb, i % fb:i % fb + 1] = returns_v[:, i * LANES:(i + 1) * LANES].astype(F32)
    row_ref[...] = (wide[...] * now_v[...] / hist_v[...]).astype(BF16).reshape(nz, nq, fb, LANES)

    pl.semaphore_wait(barrier, nz - 1 + nq - 1 + ny - 1)

    stage1 = []
    for d in far_first(nz):
        to = lax.rem(z + d, nz)
        copy = remote(row_ref.at[to], land1.at[z], send1.at[d - 1], recv1.at[d - 1], blk=to * nq + q)
        copy.start()
        stage1.append(copy)
    land1[pl.ds(z, 1)] = row_ref[pl.ds(z, 1)]

    ordered, last = sort_slots(pairs_v[...], order_v[...], me * fb)
    ordered_v[...] = ordered
    last_v[...] = last
    metas = [
        pltpu.make_async_copy(ordered_v, ordered_s, meta_sem.at[0]),
        pltpu.make_async_copy(last_v, last_s, meta_sem.at[1]),
    ]
    for copy in metas:
        copy.start()

    for copy in stage1:
        copy.wait_recv()
    stage2 = []
    for d in (4, 3, 5, 2, 6, 1, 7)[:] if nq == 8 else range(1, nq):
        to = lax.rem(q + d, nq)
        copy = remote(land1.at[:, to], gathered.at[q], send2.at[d - 1], recv2.at[d - 1], blk=z * nq + to)
        copy.start()
        stage2.append(copy)
    gathered[pl.ds(q, 1)] = land1[:, pl.ds(q, 1)].reshape(1, nz, fb, LANES)
    for copy in metas:
        copy.wait()
    for load in loads:
        load.wait()
    for copy in stage2:
        copy.wait_recv()
    by_factor = jnp.swapaxes(gathered[...].reshape(rows, fb, LANES).astype(F32), 0, 1)
    shocks_b[...] = by_factor.astype(BF16)

    unroll = min(32, slots)
    slot_bits = slots.bit_length() - 1

    def slot_group(g, carry):
        total, before = carry
        for u in range(unroll):
            j = g * unroll + u
            value = ordered_s[0, j]
            factor = value & 3
            k = (value >> 2) & (slots - 1)
            position = value >> (2 + slot_bits)
            product = jnp.dot(shocks_b[factor], sens_v[k], preferred_element_type=F32)
            same = (position == before).astype(F32)
            total = total * same + product
            running[j] = total
            before = position
        return total, before

    lax.fori_loop(0, slots // unroll, slot_group, (jnp.zeros((rows, LANES), F32), jnp.int32(-1)))

    def partial_of(p):
        value = last_s[0, p]
        return running[(value >> 1) & (slots - 1)] * (value & 1).astype(F32)

    chunks = len(dz_order)
    core_copies, x_copies, z_copies = [], [], []
    for i, dz in enumerate(dz_order):
        to_z = lax.rem(z + dz, nz)
        for to_x in range(NX):
            for h in range(2):
                give[i, to_x, h] = partial_of(((to_z * NX + to_x) * NC + (1 - c)) * 2 + h)
        copy = remote(give.at[i], got0.at[i], send_c.at[i], recv_c.at[i], blk=z * nq + x * NC + (1 - c))
        copy.start()
        core_copies.append(copy)

    right = (z * NX + lax.rem(x + 1, NX)) * NC + c
    left = (z * NX + lax.rem(x + NX - 1, NX)) * NC + c
    relays = []
    for i, dz in enumerate(dz_order):
        to_z = lax.rem(z + dz, nz)
        core_copies[i].wait_recv()
        pair = []
        for d in (2, 1, 3, 0):
            to_x = lax.rem(x + d, NX)
            for h in range(2):
                total = got0[i, to_x, h] + partial_of(((to_z * NX + to_x) * NC + c) * 2 + h)
                if d == 0:
                    mine[i, h] = total
                elif d == 2:
                    part_r[i, h] = total.astype(BF16)
                    copy = remote(
                        part_r.at[i, h], got_r.at[i, h], send_r.at[i, h], recv_r.at[i, h], blk=left if h else right
                    )
                    copy.start()
                    pair.append(copy)
                else:
                    held[i, d // 2, h] = total
        relays.append(pair)

    for i in range(chunks):
        for copy in relays[i]:
            copy.wait_recv()
        group = []
        for way in range(2):
            for h in range(2):
                total = held[i, way, h]
                if h == way:
                    total = total + got_r[i, h].astype(F32)
                part_x[i, way, h] = total.astype(BF16)
            copy = remote(
                part_x.at[i, way], got1.at[i, way], send_x.at[i, way], recv_x.at[i, way], blk=left if way else right
            )
            copy.start()
            group.append(copy)
        x_copies.append(group)

    for i, dz in enumerate(dz_order):
        for copy in x_copies[i]:
            copy.wait_recv()
        for h in range(2):
            total = mine[i, h]
            for way in range(2):
                total = total + got1[i, way, h].astype(F32)
            if dz == 0:
                mine[i, h] = total
            else:
                part_z[i, h] = total.astype(BF16)
        if dz != 0:
            copy = remote(
                part_z.at[i], got2.at[i], send_z.at[i], recv_z.at[i], blk=lax.rem(z + dz, nz) * nq + q
            )
            copy.start()
            z_copies.append(copy)
    for copy in z_copies:
        copy.wait_recv()
    for h in range(2):
        total = mine[chunks - 1, h]
        for e in range(chunks - 1):
            total = total + got2[e, h].astype(F32)
        squares[0, h:h + 1] = jnp.sum(total * total, axis=0, keepdims=True)
        total = jnp.swapaxes(total.reshape(nq, nz, LANES), 0, 1)
        out_ref[:, h * LANES:(h + 1) * LANES] = total.reshape(rows, LANES)
    y_copies = []
    for d in far_first(ny):
        copy = remote(
            squares.at[0], got3.at[d - 1], send_y.at[d - 1], recv_y.at[d - 1], scen=lax.rem(me_y + d, ny)
        )
        copy.start()
        y_copies.append(copy)
    for copy in y_copies:
        copy.wait_recv()
    total = squares[0]
    for d in range(ny - 1):
        total = total + got3[d]
    rms_ref[...] = jnp.sqrt(total / (rows * ny) + 1e-06)
    for copy in stage1 + stage2 + core_copies + z_copies + y_copies:
        copy.wait_send()
    for group in relays + x_copies:
        for copy in group:
            copy.wait_send()


def shards(ny, nz, returns, vol_hist, vol_now, sensitivity, block_pairs, book_order):
    nq = NX * NC
    slots = sensitivity.shape[0]
    blocks = book_order.shape[0]
    factors = returns.shape[1]
    rows = nz * nq
    fb = factors // (rows * LANES)
    wide = (rows, fb, LANES)
    dma = pltpu.SemaphoreType.DMA
    vm = pltpu.VMEM
    block = (rows, LANES)
    out, rms = pl.pallas_call(
        functools.partial(kernel, ny, nz, far_first(nz) + [0]),
        out_shape=(
            jax.ShapeDtypeStruct((rows, 2 * LANES), F32),
            jax.ShapeDtypeStruct((2, LANES), F32),
        ),
        in_specs=[pl.BlockSpec(memory_space=pltpu.HBM)] * 6,
        out_specs=(pl.BlockSpec(memory_space=pltpu.VMEM), pl.BlockSpec(memory_space=pltpu.VMEM)),
        scratch_shapes=[
            vm((1, factors), BF16),
            vm(wide, F32),
            vm(wide, F32),
            vm((3, slots), jnp.int32),
            vm((1, blocks), jnp.int32),
            vm(wide, F32),
            vm((nz, nq, fb, LANES), BF16),
            vm((slots, LANES, LANES), BF16),
            vm((nz, nq, fb, LANES), BF16),
            vm((nq, nz, fb, LANES), BF16),
            vm((fb,) + block, BF16),
            vm((slots,) + block, F32),
            vm((nz, NX, 2) + block, F32),
            vm((nz, NX, 2) + block, F32),
            vm((nz, 2) + block, BF16),
            vm((nz, 2) + block, BF16),
            vm((nz, 2, 2) + block, F32),
            vm((nz, 2, 2) + block, BF16),
            vm((nz, 2, 2) + block, BF16),
            vm((nz - 1, 2) + block, BF16),
            vm((nz - 1, 2) + block, BF16),
            vm((nz, 2) + block, F32),
            vm((1, 2, LANES), F32),
            vm((ny - 1, 2, LANES), F32),
            vm((1, slots), jnp.int32),
            vm((1, blocks), jnp.int32),
            pltpu.SMEM((1, slots), jnp.int32),
            pltpu.SMEM((1, blocks), jnp.int32),
            dma((5,)),
            dma((8,)),
            dma((2,)),
            dma((nz - 1,)),
            dma((nz - 1,)),
            dma((nq - 1,)),
            dma((nq - 1,)),
            dma((nz,)),
            dma((nz,)),
            dma((nz, 2)),
            dma((nz, 2)),
            dma((nz, 2)),
            dma((nz, 2)),
            dma((nz - 1,)),
            dma((nz - 1,)),
            dma((ny - 1,)),
            dma((ny - 1,)),
        ],
        compiler_params=pltpu.CompilerParams(
            collective_id=0, has_side_effects=True, vmem_limit_bytes=60 << 20
        ),
        name="profit_loss",
    )(
        returns, vol_hist.reshape(wide), vol_now.reshape(wide), block_pairs.T, book_order.reshape(1, blocks), sensitivity
    )
    return out, rms.reshape(2 * LANES)


def solution(mesh):
    ny, nb = mesh.shape["scen"], mesh.shape["blk"]
    return jax.shard_map(
        functools.partial(shards, ny, nb // (NX * NC)),
        mesh=mesh,
        in_specs=(
            P(("scen", "blk"), None),
            P(("scen", "blk"), None),
            P(),
            P("blk", None, None),
            P("blk", None),
            P(),
        ),
        out_specs=(P("scen", "blk"), P("blk")),
        check_vma=False,
    )
```

time: 61.5 us -> 51.8 us (0.84)
  the two profiles are of different devices: /device:TPU:8 before, /device:TPU:1 now
where the time goes in v2:
time: 51.8 us; the launch traced here: 51.3 us
  Pallas kernels  48 us (93%)
  local copies, waits for them, and re-layouts  2.67 us (5%)
  between operations  0.64 us (1%)
    pallas_call x1, Pallas kernels, shards(): pl.pallas_call(functools.partial(kernel, ny, nz, far_first(nz) + [0]), ou...  48 us
    unnamed x2, local copies, waits for them, and re-layouts  2.67 us

profile of v2, /device:TPU:1, one launch (start us, length us, event | category | flops | bytes accessed | tf_op | source)
XLA Modules:
  0.0 51.3 jit_solution(12795309665740969295)
XLA Ops:
  0.6 48.0 %profit_loss.1 = (f32[64,256]{1,0:T(8,128)}, f32[2,128]{1,0:T(2,128)}) custom-call(bf16[1,32768]{1,0:T(2,128)(2,1)} %returns_ref.1, f32[64,4,128]{2,1,0:T(4,128)} %bitcast.5, f32[64,4,128]{2,1,0:T(4,128)} %bitcast.6, s32[3,256]{1,0:T(4,128)} %bitcast.7, s32[1,128]{1,0:T(1,128)} %bitcast.9, bf16[256,128,128]{2,1,0:T(8,128)(2,1)} %sens_ref.1), custom_call_target="tpu_custom_call" | custom-call | tf_op jit(solution)/shard_map/profit_loss/pallas_call | solution.py:277
  48.6 1.5 %copy.10 = f32[64,256]{1,0:T(8,128)} copy(f32[64,256]{1,0:T(8,128)} %get-tuple-element.8) | data formatting | bytes 131072
  50.1 1.2 %copy.11 = f32[256]{0:T(256)} copy(f32[256]{0:T(256)} %bitcast.8) | data formatting | bytes 2048

commit v3 on v2

--- a/solution.py
+++ b/solution.py
@@ -57,11 +57,11 @@
 def kernel(
     ny, nz, dz_order,
     returns_ref, hist_ref, now_ref, pairs_ref, order_ref, sens_ref,
-    out_ref, rms_ref,
-    returns_v, hist_v, now_v, pairs_v, order_v, wide, row_ref,
-    sens_v, land1, gathered, shocks_b, running, give, got0, part_r, got_r, held, part_x, got1, part_z, got2, mine,
+    out_hbm, rms_hbm,
+    out_ref, rms_ref, returns_v, hist_v, now_v, pairs_v, order_v, wide, row_ref,
+    sens_v, land1, gathered, shocks_b, running, give, got0, part_r, got_r, held, part_x, got1, part_z, got2, mine, rest_z, got_v, rest_own, rest_mine, rest_x, got_w,
     squares, got3, ordered_v, last_v, ordered_s, last_s,
-    in_sem, sens_sem, meta_sem, send1, recv1, send2, recv2, send_c, recv_c, send_r, recv_r, send_x, recv_x, send_z, recv_z, send_y, recv_y,
+    in_sem, out_sem, sens_sem, meta_sem, send1, recv1, send2, recv2, send_c, recv_c, send_r, recv_r, send_x, recv_x, send_z, recv_z, send_v, recv_v, send_w, recv_w, send_y, recv_y,
 ):
     nq = NX * NC
     slots = sens_v.shape[0]
@@ -72,6 +72,14 @@
     x, c = q // NC, q % NC
     fb = shocks_b.shape[0]
 
+    inputs = [
+        pltpu.make_async_copy(src, dst, in_sem.at[i])
+        for i, (src, dst) in enumerate((
+            (returns_ref, returns_v), (hist_ref, hist_v), (now_ref, now_v), (pairs_ref, pairs_v), (order_ref, order_v)
+        ))
+    ]
+    for copy in inputs:
+        copy.start()
     barrier = pltpu.get_barrier_semaphore()
     for d in far_first(nz):
         pl.semaphore_signal(barrier, 1, device_id={"blk": lax.rem(z + d, nz) * nq + q}, device_id_type=MESH)
@@ -80,14 +88,6 @@
     for d in range(1, nq):
         pl.semaphore_signal(barrier, 1, device_id={"blk": z * nq + lax.rem(q + d, nq)}, device_id_type=MESH)
 
-    inputs = [
-        pltpu.make_async_copy(src, dst, in_sem.at[i])
-        for i, (src, dst) in enumerate((
-            (returns_ref, returns_v), (hist_ref, hist_v), (now_ref, now_v), (pairs_ref, pairs_v), (order_ref, order_v)
-        ))
-    ]
-    for copy in inputs:
-        copy.start()
     pieces = sens_sem.shape[0]
     each = slots // pieces
     loads = [
@@ -141,7 +141,7 @@
     by_factor = jnp.swapaxes(gathered[...].reshape(rows, fb, LANES).astype(F32), 0, 1)
     shocks_b[...] = by_factor.astype(BF16)
 
-    unroll = min(32, slots)
+    unroll = min(64, slots)
     slot_bits = slots.bit_length() - 1
 
     def slot_group(g, carry):
@@ -178,7 +178,8 @@
 
     right = (z * NX + lax.rem(x + 1, NX)) * NC + c
     left = (z * NX + lax.rem(x + NX - 1, NX)) * NC + c
-    relays = []
+    relays, rest_copies, last_copies = [], [], []
+    top = mine.shape[2]
     for i, dz in enumerate(dz_order):
         to_z = lax.rem(z + dz, nz)
         core_copies[i].wait_recv()
@@ -186,7 +187,12 @@
         for d in (2, 1, 3, 0):
             to_x = lax.rem(x + d, NX)
             for h in range(2):
-                total = got0[i, to_x, h] + partial_of(((to_z * NX + to_x) * NC + c) * 2 + h)
+                both = got0[i, to_x, h] + partial_of(((to_z * NX + to_x) * NC + c) * 2 + h)
+                total, rest = both[:top], both[top:]
+                if dz == 0:
+                    rest_own[to_x, h] = rest
+                else:
+                    rest_z[i, to_x, h] = rest.astype(BF16)
                 if d == 0:
                     mine[i, h] = total
                 elif d == 2:
@@ -198,6 +204,10 @@
                     pair.append(copy)
                 else:
                     held[i, d // 2, h] = total
+        if dz != 0:
+            copy = remote(rest_z.at[i], got_v.at[i], send_v.at[i], recv_v.at[i], blk=to_z * nq + q)
+            copy.start()
+            rest_copies.append(copy)
         relays.append(pair)
 
     for i in range(chunks):
@@ -234,15 +244,40 @@
             )
             copy.start()
             z_copies.append(copy)
-    for copy in z_copies:
+        if i == nz // 2 - 1:
+            for copy in rest_copies:
+                copy.wait_recv()
+            for d in (2, 1, 3, 0):
+                to_x = lax.rem(x + d, NX)
+                for h in range(2):
+                    total = rest_own[to_x, h]
+                    for e in range(chunks - 1):
+                        total = total + got_v[e, to_x, h].astype(F32)
+                    if d == 0:
+                        rest_mine[h] = total
+                    else:
+                        rest_x[d - 1, h] = total.astype(BF16)
+                if d > 0:
+                    copy = remote(
+                        rest_x.at[d - 1], got_w.at[d - 1], send_w.at[d - 1], recv_w.at[d - 1],
+                        blk=(z * NX + to_x) * NC + c,
+                    )
+                    copy.start()
+                    last_copies.append(copy)
+    for copy in last_copies + z_copies:
         copy.wait_recv()
     for h in range(2):
         total = mine[chunks - 1, h]
         for e in range(chunks - 1):
             total = total + got2[e, h].astype(F32)
+        rest = rest_mine[h]
+        for d in range(NX - 1):
+            rest = rest + got_w[d, h].astype(F32)
+        total = jnp.concatenate([total, rest], axis=0)
         squares[0, h:h + 1] = jnp.sum(total * total, axis=0, keepdims=True)
         total = jnp.swapaxes(total.reshape(nq, nz, LANES), 0, 1)
         out_ref[:, h * LANES:(h + 1) * LANES] = total.reshape(rows, LANES)
+    save = pltpu.make_async_copy(out_ref, out_hbm, out_sem.at[0])
     y_copies = []
     for d in far_first(ny):
         copy = remote(
@@ -250,17 +285,22 @@
         )
         copy.start()
         y_copies.append(copy)
+    save.start()
     for copy in y_copies:
         copy.wait_recv()
     total = squares[0]
     for d in range(ny - 1):
         total = total + got3[d]
     rms_ref[...] = jnp.sqrt(total / (rows * ny) + 1e-06)
-    for copy in stage1 + stage2 + core_copies + z_copies + y_copies:
+    save_rms = pltpu.make_async_copy(rms_ref, rms_hbm, out_sem.at[1])
+    save_rms.start()
+    for copy in stage1 + stage2 + core_copies + rest_copies + last_copies + z_copies + y_copies:
         copy.wait_send()
     for group in relays + x_copies:
         for copy in group:
             copy.wait_send()
+    save.wait()
+    save_rms.wait()
 
 
 def shards(ny, nz, returns, vol_hist, vol_now, sensitivity, block_pairs, book_order):
@@ -271,18 +311,20 @@
     rows = nz * nq
     fb = factors // (rows * LANES)
     wide = (rows, fb, LANES)
+    hbm = (pl.BlockSpec(memory_space=pltpu.HBM),) * 6
     dma = pltpu.SemaphoreType.DMA
     vm = pltpu.VMEM
     block = (rows, LANES)
+    upper, lower = (rows - rows // 4, LANES), (rows // 4, LANES)
+    shapes = (jax.ShapeDtypeStruct((rows, 2 * LANES), F32), jax.ShapeDtypeStruct((2, LANES), F32))
     out, rms = pl.pallas_call(
         functools.partial(kernel, ny, nz, far_first(nz) + [0]),
-        out_shape=(
-            jax.ShapeDtypeStruct((rows, 2 * LANES), F32),
-            jax.ShapeDtypeStruct((2, LANES), F32),
-        ),
-        in_specs=[pl.BlockSpec(memory_space=pltpu.HBM)] * 6,
-        out_specs=(pl.BlockSpec(memory_space=pltpu.VMEM), pl.BlockSpec(memory_space=pltpu.VMEM)),
+        out_shape=shapes,
+        in_specs=hbm,
+        out_specs=hbm[:2],
         scratch_shapes=[
+            vm((rows, 2 * LANES), F32),
+            vm((2, LANES), F32),
             vm((1, factors), BF16),
             vm(wide, F32),
             vm(wide, F32),
@@ -297,14 +339,20 @@
             vm((slots,) + block, F32),
             vm((nz, NX, 2) + block, F32),
             vm((nz, NX, 2) + block, F32),
-            vm((nz, 2) + block, BF16),
-            vm((nz, 2) + block, BF16),
-            vm((nz, 2, 2) + block, F32),
-            vm((nz, 2, 2) + block, BF16),
-            vm((nz, 2, 2) + block, BF16),
-            vm((nz - 1, 2) + block, BF16),
-            vm((nz - 1, 2) + block, BF16),
-            vm((nz, 2) + block, F32),
+            vm((nz, 2) + upper, BF16),
+            vm((nz, 2) + upper, BF16),
+            vm((nz, 2, 2) + upper, F32),
+            vm((nz, 2, 2) + upper, BF16),
+            vm((nz, 2, 2) + upper, BF16),
+            vm((nz - 1, 2) + upper, BF16),
+            vm((nz - 1, 2) + upper, BF16),
+            vm((nz, 2) + upper, F32),
+            vm((nz - 1, NX, 2) + lower, BF16),
+            vm((nz - 1, NX, 2) + lower, BF16),
+            vm((NX, 2) + lower, F32),
+            vm((2,) + lower, F32),
+            vm((NX - 1, 2) + lower, BF16),
+            vm((NX - 1, 2) + lower, BF16),
             vm((1, 2, LANES), F32),
             vm((ny - 1, 2, LANES), F32),
             vm((1, slots), jnp.int32),
@@ -312,6 +360,7 @@
             pltpu.SMEM((1, slots), jnp.int32),
             pltpu.SMEM((1, blocks), jnp.int32),
             dma((5,)),
+            dma((2,)),
             dma((8,)),
             dma((2,)),
             dma((nz - 1,)),
@@ -326,6 +375,10 @@
             dma((nz, 2)),
             dma((nz - 1,)),
             dma((nz - 1,)),
+            dma((nz - 1,)),
+            dma((nz - 1,)),
+            dma((NX - 1,)),
+            dma((NX - 1,)),
             dma((ny - 1,)),
             dma((ny - 1,)),
         ],

time: 51.8 us -> 49.7 us (0.959)
  Pallas kernels: 48 us -> 46.2 us
    pallas_call x1, Pallas kernels: 48 us -> 46.2 us  [shards(): pl.pallas_call(functools.partial(kernel, ny, nz, far_first(nz) + [0]), ou...]
where the time goes in v3:
time: 49.7 us; the launch traced here: 49.5 us
  Pallas kernels  46.2 us (93%)
  local copies, waits for them, and re-layouts  2.67 us (5%)
  between operations  0.64 us (1%)
    pallas_call x1, Pallas kernels, shards(): pl.pallas_call(functools.partial(kernel, ny, nz, far_first(nz) + [0]), ou...  46.2 us
    unnamed x2, local copies, waits for them, and re-layouts  2.67 us

profile of v3, /device:TPU:1, one launch (start us, length us, event | category | flops | bytes accessed | tf_op | source)
XLA Modules:
  0.0 49.5 jit_solution(16527570496707406080)
XLA Ops:
  0.6 46.2 %profit_loss.1 = (f32[64,256]{1,0:T(8,128)}, f32[2,128]{1,0:T(2,128)}) custom-call(bf16[1,32768]{1,0:T(2,128)(2,1)} %returns_ref.1, f32[64,4,128]{2,1,0:T(4,128)} %bitcast.5, f32[64,4,128]{2,1,0:T(4,128)} %bitcast.6, s32[3,256]{1,0:T(4,128)} %bitcast.7, s32[1,128]{1,0:T(1,128)} %bitcast.9, bf16[256,128,128]{2,1,0:T(8,128)(2,1)} %sens_ref.1), custom_call_target="tpu_custom_call" | custom-call | tf_op jit(solution)/shard_map/profit_loss/pallas_call | solution.py:320
  46.8 1.5 %copy.10 = f32[64,256]{1,0:T(8,128)} copy(f32[64,256]{1,0:T(8,128)} %get-tuple-element.8) | data formatting | bytes 131072
  48.3 1.2 %copy.11 = f32[256]{0:T(256)} copy(f32[256]{0:T(256)} %bitcast.8) | data formatting | bytes 2048

commit v4 on v3

--- a/solution.py
+++ b/solution.py
@@ -56,9 +56,9 @@
 
 def kernel(
     ny, nz, dz_order,
-    returns_ref, hist_ref, now_ref, pairs_ref, order_ref, sens_ref,
+    returns_ref, hist_ref, now_ref, slots_ref, sens_ref,
     out_hbm, rms_hbm,
-    out_ref, rms_ref, returns_v, hist_v, now_v, pairs_v, order_v, wide, row_ref,
+    out_ref, rms_ref, returns_v, hist_v, now_v, slots_v, wide, row_ref,
     sens_v, land1, gathered, shocks_b, running, give, got0, part_r, got_r, held, part_x, got1, part_z, got2, mine, rest_z, got_v, rest_own, rest_mine, rest_x, got_w,
     squares, got3, ordered_v, last_v, ordered_s, last_s,
     in_sem, out_sem, sens_sem, meta_sem, send1, recv1, send2, recv2, send_c, recv_c, send_r, recv_r, send_x, recv_x, send_z, recv_z, send_v, recv_v, send_w, recv_w, send_y, recv_y,
@@ -75,7 +75,7 @@
     inputs = [
         pltpu.make_async_copy(src, dst, in_sem.at[i])
         for i, (src, dst) in enumerate((
-            (returns_ref, returns_v), (hist_ref, hist_v), (now_ref, now_v), (pairs_ref, pairs_v), (order_ref, order_v)
+            (returns_ref, returns_v), (hist_ref, hist_v), (now_ref, now_v), (slots_ref, slots_v)
         ))
     ]
     for copy in inputs:
@@ -96,24 +96,33 @@
     ]
     for copy in inputs:
         copy.wait()
+
+    def rescale(to):
+        part = pl.ds(to * nq, nq)
+        for i in range(nq * fb):
+            start = pl.multiple_of((to * nq * fb + i) * LANES, LANES)
+            wide[i // fb, i % fb:i % fb + 1] = returns_v[:, pl.ds(start, LANES)].astype(F32)
+        row_ref[to] = (wide[...] * now_v[part] / hist_v[part]).astype(BF16)
+
+    for d in far_first(nz)[:3]:
+        rescale(lax.rem(z + d, nz))
+
+    pl.semaphore_wait(barrier, nz - 1 + nq - 1 + ny - 1)
+
+    stage1 = []
+    for n, d in enumerate(far_first(nz)):
+        to = lax.rem(z + d, nz)
+        if n > 2:
+            rescale(to)
+        copy = remote(row_ref.at[to], land1.at[z], send1.at[d - 1], recv1.at[d - 1], blk=to * nq + q)
+        copy.start()
+        stage1.append(copy)
+    rescale(z)
+    land1[pl.ds(z, 1)] = row_ref[pl.ds(z, 1)]
     for load in loads:
         load.start()
 
-    for i in range(rows * fb):
-        wide[i // fb, i % fb:i % fb + 1] = returns_v[:, i * LANES:(i + 1) * LANES].astype(F32)
-    row_ref[...] = (wide[...] * now_v[...] / hist_v[...]).astype(BF16).reshape(nz, nq, fb, LANES)
-
-    pl.semaphore_wait(barrier, nz - 1 + nq - 1 + ny - 1)
-
-    stage1 = []
-    for d in far_first(nz):
-        to = lax.rem(z + d, nz)
-        copy = remote(row_ref.at[to], land1.at[z], send1.at[d - 1], recv1.at[d - 1], blk=to * nq + q)
-        copy.start()
-        stage1.append(copy)
-    land1[pl.ds(z, 1)] = row_ref[pl.ds(z, 1)]
-
-    ordered, last = sort_slots(pairs_v[...], order_v[...], me * fb)
+    ordered, last = sort_slots(slots_v[0:3], slots_v[3:4, :last_v.shape[1]], me * fb)
     ordered_v[...] = ordered
     last_v[...] = last
     metas = [
@@ -141,7 +150,7 @@
     by_factor = jnp.swapaxes(gathered[...].reshape(rows, fb, LANES).astype(F32), 0, 1)
     shocks_b[...] = by_factor.astype(BF16)
 
-    unroll = min(64, slots)
+    unroll = min(128, slots)
     slot_bits = slots.bit_length() - 1
 
     def slot_group(g, carry):
@@ -311,7 +320,8 @@
     rows = nz * nq
     fb = factors // (rows * LANES)
     wide = (rows, fb, LANES)
-    hbm = (pl.BlockSpec(memory_space=pltpu.HBM),) * 6
+    table = jnp.pad(block_pairs.T, ((0, 1), (0, 0))) + jnp.pad(book_order[None], ((3, 0), (0, slots - blocks)))
+    hbm = (pl.BlockSpec(memory_space=pltpu.HBM),) * 5
     dma = pltpu.SemaphoreType.DMA
     vm = pltpu.VMEM
     block = (rows, LANES)
@@ -328,9 +338,8 @@
             vm((1, factors), BF16),
             vm(wide, F32),
             vm(wide, F32),
-            vm((3, slots), jnp.int32),
-            vm((1, blocks), jnp.int32),
-            vm(wide, F32),
+            vm((4, slots), jnp.int32),
+            vm((nq, fb, LANES), F32),
             vm((nz, nq, fb, LANES), BF16),
             vm((slots, LANES, LANES), BF16),
             vm((nz, nq, fb, LANES), BF16),
@@ -359,7 +368,7 @@
             vm((1, blocks), jnp.int32),
             pltpu.SMEM((1, slots), jnp.int32),
             pltpu.SMEM((1, blocks), jnp.int32),
-            dma((5,)),
+            dma((4,)),
             dma((2,)),
             dma((8,)),
             dma((2,)),
@@ -383,11 +392,11 @@
             dma((ny - 1,)),
         ],
         compiler_params=pltpu.CompilerParams(
-            collective_id=0, has_side_effects=True, vmem_limit_bytes=60 << 20
+            collective_id=0, has_side_effects=True, vmem_limit_bytes=56448000
         ),
         name="profit_loss",
     )(
-        returns, vol_hist.reshape(wide), vol_now.reshape(wide), block_pairs.T, book_order.reshape(1, blocks), sensitivity
+        returns, vol_hist.reshape(wide), vol_now.reshape(wide), table, sensitivity
     )
     return out, rms.reshape(2 * LANES)
 

time: 49.7 us -> 48.1 us (0.968)
  local copies, waits for them, and re-layouts: 2.67 us -> 1.19 us
  Pallas kernels: 46.2 us -> 45.4 us
  other arithmetic: 0 us -> 0.71 us
    unnamed x2, local copies, waits for them, and re-layouts: 2.67 us -> 1.19 us
    pallas_call x1, Pallas kernels: 46.2 us -> 45.4 us  [shards(): pl.pallas_call(functools.partial(kernel, ny, nz, far_first(nz) + [0]), ou...]
    add x0 -> x1, other arithmetic: none -> 0.71 us  [shards(): jnp.pad(block_pairs.T, ((0, 1), (0, 0)))]
where the time goes in v4:
time: 48.1 us; the launch traced here: 48 us
  Pallas kernels  45.4 us (94%)
  local copies, waits for them, and re-layouts  1.19 us (2%)
  other arithmetic  0.71 us (1%)
  between operations  0.64 us (1%)
    pallas_call x1, Pallas kernels, shards(): pl.pallas_call(functools.partial(kernel, ny, nz, far_first(nz) + [0]), ou...  45.4 us
    unnamed x2, local copies, waits for them, and re-layouts  1.19 us

profile of v4, /device:TPU:1, one launch (start us, length us, event | category | flops | bytes accessed | tf_op | source)
XLA Modules:
  0.0 48.0 jit_solution(233416999554518537)
XLA Ops:
  0.6 0.7 %pad_add_fusion.slots_ref = s32[4,256]{1,0:T(4,128)S(1)} fusion(s32[1,128]{1,0:T(1,128)} %bitcast.9, s32[3,256]{1,0:T(4,128)} %bitcast.8), kind=kLoop, calls=%fused_computation | loop fusion | flops 1024 | bytes 7680 | tf_op jit(solution)/shard_map/add | solution.py:323
  1.3 45.4 %profit_loss.1 = (f32[64,256]{1,0:T(8,128)S(1)}, f32[2,128]{1,0:T(2,128)S(1)}) custom-call(bf16[1,32768]{1,0:T(2,128)(2,1)} %returns_ref.1, f32[64,4,128]{2,1,0:T(4,128)} %bitcast.6, f32[64,4,128]{2,1,0:T(4,128)} %bitcast.7, s32[4,256]{1,0:T(4,128)S(1)} %pad_add_fusion.slots_ref, bf16[256,128,128]{2,1,0:T(8,128)(2,1)} %sens_ref.1), custom_call_target="tpu_custom_call" | custom-call | tf_op jit(solution)/shard_map/profit_loss/pallas_call | solution.py:330
  46.8 0.6 %copy.10 = f32[64,256]{1,0:T(8,128)} copy(f32[64,256]{1,0:T(8,128)S(1)} %get-tuple-element.8) | data formatting | bytes 131072
  47.4 0.6 %copy.11 = f32[256]{0:T(256)} copy(f32[256]{0:T(256)S(1)} %bitcast.5) | data formatting | bytes 2048

commit v5 on v4

--- a/solution.py
+++ b/solution.py
@@ -57,11 +57,11 @@
 def kernel(
     ny, nz, dz_order,
     returns_ref, hist_ref, now_ref, slots_ref, sens_ref,
-    out_hbm, rms_hbm,
-    out_ref, rms_ref, returns_v, hist_v, now_v, slots_v, wide, row_ref,
+    out_ref, rms_ref,
+    returns_v, hist_v, now_v, slots_v, wide, row_ref,
     sens_v, land1, gathered, shocks_b, running, give, got0, part_r, got_r, held, part_x, got1, part_z, got2, mine, rest_z, got_v, rest_own, rest_mine, rest_x, got_w,
     squares, got3, ordered_v, last_v, ordered_s, last_s,
-    in_sem, out_sem, sens_sem, meta_sem, send1, recv1, send2, recv2, send_c, recv_c, send_r, recv_r, send_x, recv_x, send_z, recv_z, send_v, recv_v, send_w, recv_w, send_y, recv_y,
+    in_sem, sens_sem, meta_sem, send1, recv1, send2, recv2, send_c, recv_c, send_r, recv_r, send_x, recv_x, send_z, recv_z, send_v, recv_v, send_w, recv_w, send_y, recv_y,
 ):
     nq = NX * NC
     slots = sens_v.shape[0]
@@ -286,7 +286,6 @@
         squares[0, h:h + 1] = jnp.sum(total * total, axis=0, keepdims=True)
         total = jnp.swapaxes(total.reshape(nq, nz, LANES), 0, 1)
         out_ref[:, h * LANES:(h + 1) * LANES] = total.reshape(rows, LANES)
-    save = pltpu.make_async_copy(out_ref, out_hbm, out_sem.at[0])
     y_copies = []
     for d in far_first(ny):
         copy = remote(
@@ -294,22 +293,17 @@
         )
         copy.start()
         y_copies.append(copy)
-    save.start()
+    for copy in stage1 + stage2 + core_copies + rest_copies + last_copies + z_copies + y_copies:
+        copy.wait_send()
+    for group in relays + x_copies:
+        for copy in group:
+            copy.wait_send()
     for copy in y_copies:
         copy.wait_recv()
     total = squares[0]
     for d in range(ny - 1):
         total = total + got3[d]
     rms_ref[...] = jnp.sqrt(total / (rows * ny) + 1e-06)
-    save_rms = pltpu.make_async_copy(rms_ref, rms_hbm, out_sem.at[1])
-    save_rms.start()
-    for copy in stage1 + stage2 + core_copies + rest_copies + last_copies + z_copies + y_copies:
-        copy.wait_send()
-    for group in relays + x_copies:
-        for copy in group:
-            copy.wait_send()
-    save.wait()
-    save_rms.wait()
 
 
 def shards(ny, nz, returns, vol_hist, vol_now, sensitivity, block_pairs, book_order):
@@ -331,10 +325,8 @@
         functools.partial(kernel, ny, nz, far_first(nz) + [0]),
         out_shape=shapes,
         in_specs=hbm,
-        out_specs=hbm[:2],
+        out_specs=(pl.BlockSpec(memory_space=pltpu.VMEM),) * 2,
         scratch_shapes=[
-            vm((rows, 2 * LANES), F32),
-            vm((2, LANES), F32),
             vm((1, factors), BF16),
             vm(wide, F32),
             vm(wide, F32),
@@ -369,7 +361,6 @@
             pltpu.SMEM((1, slots), jnp.int32),
             pltpu.SMEM((1, blocks), jnp.int32),
             dma((4,)),
-            dma((2,)),
             dma((8,)),
             dma((2,)),
             dma((nz - 1,)),

time: 48.1 us -> 48 us (level)
  no operation moved by 1% of the time
where the time goes in v5:
time: 48 us; the launch traced here: 47.8 us
  Pallas kernels  45.3 us (94%)
  local copies, waits for them, and re-layouts  1.19 us (2%)
  other arithmetic  0.71 us (1%)
  between operations  0.64 us (1%)
    pallas_call x1, Pallas kernels, shards(): pl.pallas_call(functools.partial(kernel, ny, nz, far_first(nz) + [0]), ou...  45.3 us
    unnamed x2, local copies, waits for them, and re-layouts  1.19 us

profile of v5, /device:TPU:1, one launch (start us, length us, event | category | flops | bytes accessed | tf_op | source)
XLA Modules:
  0.0 47.8 jit_solution(10991928799825303837)
XLA Ops:
  0.6 0.7 %pad_add_fusion.slots_ref = s32[4,256]{1,0:T(4,128)S(1)} fusion(s32[1,128]{1,0:T(1,128)} %bitcast.9, s32[3,256]{1,0:T(4,128)} %bitcast.8), kind=kLoop, calls=%fused_computation | loop fusion | flops 1024 | bytes 7680 | tf_op jit(solution)/shard_map/add | solution.py:317
  1.3 45.3 %profit_loss.1 = (f32[64,256]{1,0:T(8,128)S(1)}, f32[2,128]{1,0:T(2,128)S(1)}) custom-call(bf16[1,32768]{1,0:T(2,128)(2,1)} %returns_ref.1, f32[64,4,128]{2,1,0:T(4,128)} %bitcast.6, f32[64,4,128]{2,1,0:T(4,128)} %bitcast.7, s32[4,256]{1,0:T(4,128)S(1)} %pad_add_fusion.slots_ref, bf16[256,128,128]{2,1,0:T(8,128)(2,1)} %sens_ref.1), custom_call_target="tpu_custom_call" | custom-call | tf_op jit(solution)/shard_map/profit_loss/pallas_call | solution.py:324
  46.6 0.6 %copy.10 = f32[64,256]{1,0:T(8,128)} copy(f32[64,256]{1,0:T(8,128)S(1)} %get-tuple-element.8) | data formatting | bytes 131072
  47.3 0.6 %copy.11 = f32[256]{0:T(256)} copy(f32[256]{0:T(256)S(1)} %bitcast.5) | data formatting | bytes 2048
